TPU v7x, 32 devices: a whole 2x2x4 slice. The times are simulated.
32 devices in a mesh: seq: 4 (over y, x), fsdp: 8 (over z, core).
Axes of the slice: x: 2, y: 2, z: 4, core: 2. Of those that a mesh axis runs over, the one named last changes fastest.
Arguments:
- tokens: bfloat16 [8, 512, 2048], P('fsdp', 'seq'), may hold values from -6 to 6
- documents: int32 [8, 512], P('fsdp'), may hold values from 0 to 3, never falling along the last dimension, each value on 1 to 256 neighbouring positions
- cotangent: bfloat16 [8, 512, 2048], P('fsdp', 'seq'), may hold values from -6 to 6
- w_query: bfloat16 [2048, 2048], P('fsdp'), may hold values from -2.5 to 2.5
- w_key: bfloat16 [2048, 512], P('fsdp'), may hold values from -1 to 1
- w_value: bfloat16 [2048, 512], P('fsdp'), may hold values from -0.125 to 0.125
- w_output: bfloat16 [2048, 2048], P('fsdp'), may hold values from -0.5 to 0.5
- w_gate: bfloat16 [2048, 8192], P('fsdp'), may hold values from -0.125 to 0.125
- w_up: bfloat16 [2048, 8192], P('fsdp'), may hold values from -0.125 to 0.125
- w_down: bfloat16 [8192, 2048], P('fsdp'), may hold values from -0.0625 to 0.0625
- gain_attn: bfloat16 [2048], P('fsdp'), may hold values from 0.25 to 1.75
- gain_mlp: bfloat16 [2048], P('fsdp'), may hold values from 0.25 to 1.75
Outputs:
- output: bfloat16 [8, 512, 2048], P('fsdp', 'seq')
- grad_tokens: bfloat16 [8, 512, 2048], P('fsdp', 'seq')
- grad_w_query: float32 [2048, 2048], P('fsdp')
- grad_w_key: float32 [2048, 512], P('fsdp')
- grad_w_value: float32 [2048, 512], P('fsdp')
- grad_w_output: float32 [2048, 2048], P('fsdp')
- grad_w_gate: float32 [2048, 8192], P('fsdp')
- grad_w_up: float32 [2048, 8192], P('fsdp')
- grad_w_down: float32 [8192, 2048], P('fsdp')
- grad_gain_attn: float32 [2048], P('fsdp')
- grad_gain_mlp: float32 [2048], P('fsdp')
Inputs may be any that keep to these rules, and one draw needn't show every extreme that they name: Each sequence holds 4 documents numbered in order, each of 1 to 256 tokens, one exactly 256 long.
All inputs are finite; a program needn't handle non-finite values.
Results may differ from a plain program's by a relative error of at most 0.02.
Values may be sent and summed in bfloat16 or wider, within the bound.
No kernel may reach another device: no remote copies, remote signals or barrier semaphores. Data moves between devices by JAX's collectives and lax.ppermute only.
A program may use at most 512 MiB of HBM per device.

v0:
```python
import math

import jax
import jax.numpy as jnp
from jax import lax
from jax.sharding import PartitionSpec as P

HD = 64


EPSILON = 1e-05
NEGATIVE = -1e30


def shortened(shard):
    return jax.tree.map(lambda a: a.astype(jnp.bfloat16) if a.dtype == jnp.float32 else a, shard)


def frequencies():
    base_rate = 500000.0 ** (-jnp.arange(0, HD, 2, dtype=jnp.float32) / HD)
    wavelength = 2.0 * math.pi / base_rate
    smooth = (8192.0 / wavelength - 1.0) / 3.0
    middle_rate = (1.0 - smooth) * base_rate / 32.0 + smooth * base_rate
    return jnp.where(
        wavelength > 8192.0,
        base_rate / 32.0,
        jnp.where(wavelength < 2048.0, base_rate, middle_rate),
    )


def positions(doc_ids):
    index_all = jnp.arange(doc_ids.shape[0], dtype=jnp.int32)
    fresh = jnp.concatenate([jnp.ones((1,), dtype=bool), doc_ids[1:] != doc_ids[:-1]])
    first_index = lax.cummax(jnp.where(fresh, index_all, jnp.zeros_like(index_all)), axis=0)
    return index_all - first_index


def tables(pos_values):
    angles = pos_values.astype(jnp.float32)[:, None] * frequencies()[None, :]
    return (
        jnp.concatenate([jnp.cos(angles)] * 2, axis=1),
        jnp.concatenate([jnp.sin(angles)] * 2, axis=1),
    )


def rotation(values, cosine_table, sine_table):
    row_count = values.shape[0]
    shaped = values.reshape(row_count, -1, HD)
    half_size = HD // 2
    turned = jnp.concatenate([-shaped[..., half_size:], shaped[..., :half_size]], axis=-1)
    return (shaped * cosine_table[:, None, :] + turned * sine_table[:, None, :]).reshape(
        row_count, -1
    )


def product(left_side, right_side):
    return jnp.dot(left_side, right_side, preferred_element_type=jnp.float32)


def product_back(left_side, right_side):
    return lax.dot_general(
        left_side, right_side, (((1,), (1,)), ((), ())), preferred_element_type=jnp.float32
    )


def outer_rows(left_side, right_side):
    return lax.dot_general(
        left_side, right_side, (((0,), (0,)), ((), ())), preferred_element_type=jnp.float32
    )


def norm_factor(values):
    return lax.rsqrt(jnp.mean(values * values, axis=-1, keepdims=True) + EPSILON)


def norm_back(grad_normed, normed, factor):
    return factor * (grad_normed - normed * jnp.mean(grad_normed * normed, axis=-1, keepdims=True))


def visible_mask(doc_ids, block_start, block_rows):
    total_len = doc_ids.shape[0]
    row_index = block_start + jnp.arange(block_rows, dtype=jnp.int32)
    column_index = jnp.arange(total_len, dtype=jnp.int32)
    row_docs = lax.dynamic_slice_in_dim(doc_ids, block_start, block_rows)
    return (column_index[None, :] <= row_index[:, None]) & (row_docs[:, None] == doc_ids[None, :])


def head_layout(query_heads, key_heads, value_heads):
    total_len = query_heads.shape[0]
    kv_local = key_heads.shape[1] // HD
    group_size = query_heads.shape[1] // key_heads.shape[1]
    queries = query_heads.reshape(total_len, kv_local, group_size, HD)
    keys_all = key_heads.reshape(total_len, kv_local, HD)
    values_all = value_heads.reshape(total_len, kv_local, HD)
    block_rows = 512
    return (queries, keys_all, values_all, block_rows)


def block_scores(query_block, keys_all, doc_ids, block_start, block_rows):
    scores = jnp.einsum(
        "qhgd,khd->hgqk", query_block, keys_all, preferred_element_type=jnp.float32
    ) * HD ** (-0.5)
    return jnp.where(visible_mask(doc_ids, block_start, block_rows)[None, None], scores, NEGATIVE)


def attend_forward(query_heads, key_heads, value_heads, doc_ids):
    total_len = query_heads.shape[0]
    queries, keys_all, values_all, block_rows = head_layout(query_heads, key_heads, value_heads)

    def one_block(block_index):
        block_start = block_index * block_rows
        query_block = lax.dynamic_slice_in_dim(queries, block_start, block_rows, 0)
        scores = block_scores(query_block, keys_all, doc_ids, block_start, block_rows)
        largest = jnp.max(scores, axis=-1, keepdims=True)
        log_total = largest + jnp.log(jnp.sum(jnp.exp(scores - largest), axis=-1, keepdims=True))
        probs_low = jnp.exp(scores - log_total).astype(jnp.bfloat16)
        mixed_block = jnp.einsum(
            "hgqk,khd->qhgd", probs_low, values_all, preferred_element_type=jnp.float32
        )
        return (mixed_block.reshape(block_rows, -1), log_total)

    mixed_blocks, log_totals = lax.map(
        one_block, jnp.arange(total_len // block_rows, dtype=jnp.int32)
    )
    return (mixed_blocks.reshape(total_len, -1), log_totals)


def attend_backward(query_heads, key_heads, value_heads, grad_heads, log_totals, doc_ids):
    total_len = query_heads.shape[0]
    queries, keys_all, values_all, block_rows = head_layout(query_heads, key_heads, value_heads)
    grads_out = grad_heads.reshape(queries.shape)
    factor = HD ** (-0.5)

    def one_block(carry_sums, block_index):
        key_sum, value_sum = carry_sums
        block_start = block_index * block_rows
        query_block = lax.dynamic_slice_in_dim(queries, block_start, block_rows, 0)
        grad_block = lax.dynamic_slice_in_dim(grads_out, block_start, block_rows, 0)
        scores = block_scores(query_block, keys_all, doc_ids, block_start, block_rows)
        probs = jnp.exp(scores - log_totals[block_index])
        probs_low = probs.astype(jnp.bfloat16)
        grad_probs = jnp.einsum(
            "qhgd,khd->hgqk", grad_block, values_all, preferred_element_type=jnp.float32
        )
        centre = jnp.sum(probs * grad_probs, axis=-1, keepdims=True)
        grad_scores = (probs * (grad_probs - centre)).astype(jnp.bfloat16)
        query_grad = (
            jnp.einsum("hgqk,khd->qhgd", grad_scores, keys_all, preferred_element_type=jnp.float32)
            * factor
        )
        key_sum = (
            key_sum
            + jnp.einsum(
                "hgqk,qhgd->khd", grad_scores, query_block, preferred_element_type=jnp.float32
            )
            * factor
        )
        value_sum = value_sum + jnp.einsum(
            "hgqk,qhgd->khd", probs_low, grad_block, preferred_element_type=jnp.float32
        )
        return ((key_sum, value_sum), query_grad.reshape(block_rows, -1))

    zero_sums = jnp.zeros(keys_all.shape, jnp.float32)
    sums, query_grads = lax.scan(
        one_block, (zero_sums, zero_sums), jnp.arange(total_len // block_rows, dtype=jnp.int32)
    )
    return (
        query_grads.reshape(total_len, -1).astype(jnp.bfloat16),
        sums[0].reshape(total_len, -1).astype(jnp.bfloat16),
        sums[1].reshape(total_len, -1).astype(jnp.bfloat16),
    )


def shards(
    tokens,
    documents,
    cotangent,
    w_query,
    w_key,
    w_value,
    w_output,
    w_gate,
    w_up,
    w_down,
    gain_attn,
    gain_mlp,
):
    own_rows = tokens.shape[1]
    width = tokens.shape[2]
    hidden_width = w_gate.shape[1]
    inputs = tokens.reshape(own_rows, width).astype(jnp.float32)
    doc_ids = documents.reshape(-1)
    own_start = lax.axis_index("seq") * own_rows
    cosine_table, sine_table = tables(
        lax.dynamic_slice_in_dim(positions(doc_ids), own_start, own_rows)
    )
    attn_full = (
        lax.all_gather(w_query, "fsdp", axis=0, tiled=True),
        lax.all_gather(w_key, "fsdp", axis=0, tiled=True),
        lax.all_gather(w_value, "fsdp", axis=0, tiled=True),
        lax.all_gather(w_output, "fsdp", axis=0, tiled=True),
        lax.all_gather(gain_attn, "fsdp", axis=0, tiled=True),
        lax.all_gather(gain_mlp, "fsdp", axis=0, tiled=True),
    )
    full_query, full_key, full_value, full_output, full_gain_attn, full_gain_mlp = attn_full
    scale_one = norm_factor(inputs)
    normed_one = inputs * scale_one
    normed_low = (normed_one * full_gain_attn.astype(jnp.float32)).astype(jnp.bfloat16)
    query_send = rotation(product(normed_low, full_query), cosine_table, sine_table).astype(
        jnp.bfloat16
    )
    key_send = rotation(product(normed_low, full_key), cosine_table, sine_table).astype(
        jnp.bfloat16
    )
    value_send = product(normed_low, full_value).astype(jnp.bfloat16)
    query_heads, key_heads, value_heads = (
        lax.all_to_all(query_send, "seq", split_axis=1, concat_axis=0, tiled=True),
        lax.all_to_all(key_send, "seq", split_axis=1, concat_axis=0, tiled=True),
        lax.all_to_all(value_send, "seq", split_axis=1, concat_axis=0, tiled=True),
    )
    mixed_heads, log_totals = attend_forward(query_heads, key_heads, value_heads, doc_ids)
    mixed_tokens = lax.all_to_all(
        mixed_heads.astype(jnp.bfloat16), "seq", split_axis=0, concat_axis=1, tiled=True
    )
    middle = inputs + product(mixed_tokens, full_output)
    scale_two = norm_factor(middle)
    normed_two = middle * scale_two
    normed_two_low = (normed_two * full_gain_mlp.astype(jnp.float32)).astype(jnp.bfloat16)
    paired_rows = jnp.concatenate([w_gate, w_up], axis=1)
    paired = product(normed_two_low, lax.all_gather(paired_rows, "fsdp", axis=0, tiled=True))
    gate = paired[:, :hidden_width]
    upward = paired[:, hidden_width:]
    sigmoid_gate = jax.nn.sigmoid(gate)
    activated = gate * sigmoid_gate
    hidden = (activated * upward).astype(jnp.bfloat16)
    full_down = lax.all_gather(w_down, "fsdp", axis=0, tiled=True)
    output = (middle + product(hidden, full_down)).astype(jnp.bfloat16)
    upstream = cotangent.reshape(own_rows, width).astype(jnp.float32)
    upstream_low = upstream.astype(jnp.bfloat16)
    grad_hidden = product_back(upstream_low, full_down)
    grad_up = (grad_hidden * activated).astype(jnp.bfloat16)
    grad_gate = (grad_hidden * upward * sigmoid_gate * (1.0 + gate * (1.0 - sigmoid_gate))).astype(
        jnp.bfloat16
    )
    grad_paired = jnp.concatenate([grad_gate, grad_up], axis=1)
    grad_normed_two = product_back(
        grad_paired, lax.all_gather(paired_rows, "fsdp", axis=0, tiled=True)
    )
    gain_two_grad = jnp.sum(grad_normed_two * normed_two, axis=0)
    grad_middle = upstream + norm_back(
        grad_normed_two * full_gain_mlp.astype(jnp.float32), normed_two, scale_two
    )
    middle_low = grad_middle.astype(jnp.bfloat16)
    grad_send = product_back(middle_low, full_output).astype(jnp.bfloat16)
    grad_heads = lax.all_to_all(grad_send, "seq", split_axis=1, concat_axis=0, tiled=True)
    query_grad, key_grad, value_grad = attend_backward(
        query_heads, key_heads, value_heads, grad_heads, log_totals, doc_ids
    )
    query_back, key_back, value_back = (
        lax.all_to_all(query_grad, "seq", split_axis=0, concat_axis=1, tiled=True),
        lax.all_to_all(key_grad, "seq", split_axis=0, concat_axis=1, tiled=True),
        lax.all_to_all(value_grad, "seq", split_axis=0, concat_axis=1, tiled=True),
    )
    query_raw_grad = rotation(query_back.astype(jnp.float32), cosine_table, -sine_table).astype(
        jnp.bfloat16
    )
    key_raw_grad = rotation(key_back.astype(jnp.float32), cosine_table, -sine_table).astype(
        jnp.bfloat16
    )
    grad_normed_one = (
        product_back(query_raw_grad, full_query)
        + product_back(key_raw_grad, full_key)
        + product_back(value_back, full_value)
    )
    gain_one_grad = jnp.sum(grad_normed_one * normed_one, axis=0)
    input_grad = grad_middle + norm_back(
        grad_normed_one * full_gain_attn.astype(jnp.float32), normed_one, scale_one
    )
    attn_terms = (
        outer_rows(normed_low, query_raw_grad),
        outer_rows(normed_low, key_raw_grad),
        outer_rows(normed_low, value_back),
        outer_rows(mixed_tokens, middle_low),
        gain_one_grad,
        gain_two_grad,
    )
    attn_owned = tuple(
        (
            lax.psum_scatter(
                attn_terms[0].astype(jnp.bfloat16), "fsdp", scatter_dimension=0, tiled=True
            ).astype(jnp.float32),
            lax.psum_scatter(
                attn_terms[1].astype(jnp.bfloat16), "fsdp", scatter_dimension=0, tiled=True
            ).astype(jnp.float32),
            lax.psum_scatter(
                attn_terms[2].astype(jnp.bfloat16), "fsdp", scatter_dimension=0, tiled=True
            ).astype(jnp.float32),
            lax.psum_scatter(
                attn_terms[3].astype(jnp.bfloat16), "fsdp", scatter_dimension=0, tiled=True
            ).astype(jnp.float32),
            lax.psum_scatter(
                attn_terms[4].astype(jnp.bfloat16), "fsdp", scatter_dimension=0, tiled=True
            ).astype(jnp.float32),
            lax.psum_scatter(
                attn_terms[5].astype(jnp.bfloat16), "fsdp", scatter_dimension=0, tiled=True
            ).astype(jnp.float32),
        )
    )
    down_owned = lax.psum_scatter(
        outer_rows(hidden, upstream_low).astype(jnp.bfloat16),
        "fsdp",
        scatter_dimension=0,
        tiled=True,
    ).astype(jnp.float32)
    finished = ()
    pending = (
        lax.psum_scatter(
            outer_rows(normed_two_low, grad_paired).astype(jnp.bfloat16),
            "fsdp",
            scatter_dimension=0,
            tiled=True,
        ).astype(jnp.float32),
    )
    summed = jax.tree.map(
        lambda part: part.astype(jnp.float32),
        lax.psum(shortened(attn_owned + (down_owned,) + pending), "seq"),
    )
    paired_owned = (finished + tuple(summed[7:]))[0]
    return (
        output.reshape(1, own_rows, width),
        input_grad.astype(jnp.bfloat16).reshape(1, own_rows, width),
        summed[0],
        summed[1],
        summed[2],
        summed[3],
        paired_owned[:, :hidden_width],
        paired_owned[:, hidden_width:],
        summed[6],
        summed[4],
        summed[5],
    )


def solution(mesh):
    return jax.shard_map(
        shards,
        mesh=mesh,
        in_specs=(
            P("fsdp", "seq", None),
            P("fsdp", None),
            P("fsdp", "seq", None),
            P("fsdp", None),
            P("fsdp", None),
            P("fsdp", None),
            P("fsdp", None),
            P("fsdp", None),
            P("fsdp", None),
            P("fsdp", None),
            P("fsdp"),
            P("fsdp"),
        ),
        out_specs=(
            P("fsdp", "seq", None),
            P("fsdp", "seq", None),
            P("fsdp", None),
            P("fsdp", None),
            P("fsdp", None),
            P("fsdp", None),
            P("fsdp", None),
            P("fsdp", None),
            P("fsdp", None),
            P("fsdp"),
            P("fsdp"),
        ),
        check_vma=False,
    )
```

profile of v0, /device:TPU:0, one launch (start us, length us, event | category | flops | bytes accessed | tf_op | source)
XLA Modules:
  0.0 2720.9 jit_solution(824376886688379923)
XLA Ops:
  10.0 7.7 pad_maximum_fusion
  18.4 13.5 all-gather
  33.3 8.2 all-gather.11.cloned.1.call-done
  49.6 22.1 all-gather.9.cloned.1.call-done
  74.5 80.4 %all-gather.13.cloned.1.call-done = bf16[2048,2048]{1,0:T(8,128)(2,1)} async-done(((bf16[256,2048]{1,0:T(8,128)(2,1)}), bf16[2048,2048]{1,0:T(8,128)(2,1)}) %all-gather.13.cloned.1.call-update) | async-done | bytes 8388624 | tf_op jit(solution)/shard_map/all_gather | solution.py:198
  154.9 12.3 copy.53
  186.2 7.1 all-to-all-done.2
  205.7 10.1 all-gather.1
  215.8 21.3 all-gather.15.cloned.1.call-done
  241.8 559.8 %all-gather.17.cloned.1.call-done = bf16[2048,16384]{1,0:T(8,128)(2,1)} async-done(((bf16[256,16384]{1,0:T(8,128)(2,1)}), bf16[2048,16384]{1,0:T(8,128)(2,1)}) %all-gather.17.cloned.1.call-update) | async-done | bytes 67108880 | tf_op jit(solution)/shard_map/all_gather | solution.py:230
  801.6 31.8 %fusion.70 = f32[128,16384]{1,0:T(8,128)} fusion(bf16[2048,16384]{1,0:T(8,128)(2,1)} %all-gather.17.cloned.1.call-done, f32[128,2048]{1,0:T(8,128)S(1)} %get-tuple-element.106, f32[2048]{0:T(1024)S(1)} %bitcast.244, f32[128]{0:T(128)S(1)} %add_rsqrt_fusion), kind=kOutput, calls=%fused_computation.133 | convolution fusion | flops 8590721024 | bytes 76554752 | tf_op jit(solution)/shard_map/dot_general | solution.py:57
  833.4 256.5 %all-gather.19.cloned.1.call-done = bf16[8192,2048]{1,0:T(8,128)(2,1)} async-done(((bf16[1024,2048]{1,0:T(8,128)(2,1)}), bf16[8192,2048]{1,0:T(8,128)(2,1)}) %all-gather.19.cloned.1.call-update) | async-done | bytes 33554448 | tf_op jit(solution)/shard_map/all_gather | solution.py:236
  1089.9 21.0 multiply_convert_fusion.1
  1110.9 29.9 %multiply_reduce_fusion = (bf16[2048]{0:T(1024)(128)(2,1)S(1)}, f32[128]{0:T(128)S(1)}, f32[128,2048]{1,0:T(8,128)}) fusion(f32[128,2048]{1,0:T(8,128)S(1)} %get-tuple-element.106, f32[128]{0:T(128)S(1)} %add_rsqrt_fusion, f32[2048]{0:T(1024)S(1)} %bitcast.245, bf16[2048,16384]{1,0:T(8,128)(2,1)} %all-gather.17.cloned.1.call-done, ...), kind=kOutput, calls=%fused_computation.70 | convolution fusion | flops 8599894016 | bytes 73413632 | tf_op jit(solution)/shard_map/dot_general | solution.py:61
  1148.8 12.5 all_to_all.110
  1165.5 6.3 fusion.22
  1174.3 7.4 all_to_all.111
  1184.6 6.6 fusion
  1199.4 7.4 all_to_all.112
  1221.4 9.7 all_to_all.113
  1238.5 15.7 convolution_convert_fusion.1
  1254.3 27.8 %convolution_convert_fusion = bf16[2048,16384]{1,0:T(8,128)(2,1)} fusion(bf16[128,8192]{1,0:T(8,128)(2,1)} %get-tuple-element.87, bf16[128,8192]{1,0:T(8,128)(2,1)} %get-tuple-element.86, f32[128,2048]{1,0:T(8,128)S(1)} %get-tuple-element.106, f32[2048]{0:T(1024)S(1)} %bitcast.247, f32[128]{0:T(128)S(1)} %add_rsqrt_fusion), kind=kOutput, calls=%fused_computation | convolution fusion | flops 8632664064 | bytes 72360448 | tf_op jit(solution)/shard_map/dot_general | solution.py:67
  1282.4 63.4 %reduce-scatter.13.cloned.1.call-done = bf16[256,2048]{1,0:T(8,128)(2,1)} async-done(((bf16[2048,2048]{1,0:T(8,128)(2,1)}), bf16[256,2048]{1,0:T(8,128)(2,1)}) %reduce-scatter.13.cloned.1.call-update) | async-done | bytes 1048592 | tf_op jit(solution)/shard_map/reduce_scatter | solution.py:298
  1345.9 90.7 %reduce-scatter.7.cloned.1.call-done = bf16[256,2048]{1,0:T(8,128)(2,1)} async-done(((bf16[2048,2048]{1,0:T(8,128)(2,1)}), bf16[256,2048]{1,0:T(8,128)(2,1)}) %reduce-scatter.7.cloned.1.call-update) | async-done | bytes 1048592 | tf_op jit(solution)/shard_map/reduce_scatter | solution.py:289
  1436.6 326.3 %reduce-scatter.17.cloned.1.call-done = bf16[1024,2048]{1,0:T(8,128)(2,1)} async-done(((bf16[8192,2048]{1,0:T(8,128)(2,1)}), bf16[1024,2048]{1,0:T(8,128)(2,1)}) %reduce-scatter.17.cloned.1.call-update) | async-done | bytes 4194320 | tf_op jit(solution)/shard_map/reduce_scatter | solution.py:309
  1762.9 640.9 %reduce-scatter.15.cloned.1.call-done = bf16[256,16384]{1,0:T(8,128)(2,1)} async-done(((bf16[2048,16384]{1,0:T(8,128)(2,1)}), bf16[256,16384]{1,0:T(8,128)(2,1)}) %reduce-scatter.15.cloned.1.call-update) | async-done | bytes 8388624 | tf_op jit(solution)/shard_map/reduce_scatter | solution.py:317
  2405.1 17.8 fusion.8
  2423.1 6.5 fusion.77
  2431.5 13.9 all-reduce.2
  2445.6 10.5 all-reduce.3
  2458.4 234.2 %all-reduce.7.cloned.1.call-done = (bf16[256,2048]{1,0:T(8,128)(2,1)}, bf16[256,512]{1,0:T(8,128)(2,1)}, bf16[256,512]{1,0:T(8,128)(2,1)}, bf16[256,2048]{1,0:T(...) async-done(((bf16[256,2048]{1,0:T(8,128)(2,1)}, bf16[256,512]{1,0:T(8,128)(2,1)}, bf16[256,512]{1,0:T(8,128)(2,1)}, bf16[256,2048]{1,0:T(8,128)(2,1)}, ...) | async-done | bytes 15204368 | tf_op jit(solution)/shard_map/psum | solution.py:326
  2692.6 12.0 fusion.76
  (168 shorter events, 113.8 us)
Async XLA Ops:
  7.2 34.3 %all-gather.11.cloned.1.call-start = ((), (), s32[]{:S(2)}) async-start(), calls=%async_computation.15 | async-start | bytes 2359296 | tf_op jit(solution)/shard_map/all_gather | solution.py:199
  7.9 63.8 %all-gather.9.cloned.1.call-start = ((), (), s32[]{:S(2)}) async-start(), calls=%async_computation.14 | async-start | bytes 2359296 | tf_op jit(solution)/shard_map/all_gather | solution.py:200
  8.7 146.3 %all-gather.13.cloned.1.call-start = ((), (), s32[]{:S(2)}) async-start(), calls=%async_computation.16 | async-start | bytes 9437184 | tf_op jit(solution)/shard_map/all_gather | solution.py:198
  9.4 227.7 %all-gather.15.cloned.1.call-start = ((), (), s32[]{:S(2)}) async-start(), calls=%async_computation.17 | async-start | bytes 9437184 | tf_op jit(solution)/shard_map/all_gather | solution.py:201
  10.0 791.6 %all-gather.17.cloned.1.call-start = ((), (), s32[]{:S(2)}) async-start(), calls=%async_computation.18 | async-start | bytes 75497472 | tf_op jit(solution)/shard_map/all_gather | solution.py:230
  17.8 14.2 copy-start.21
  17.8 15.3 copy-start.1
  17.8 1072.1 %all-gather.19.cloned.1.call-start = ((), (), s32[]{:S(2)}) async-start(), calls=%async_computation.19 | async-start | bytes 37748736 | tf_op jit(solution)/shard_map/all_gather | solution.py:236
  46.0 127.2 %all-to-all-start.1 = ((bf16[128,4,128]{0,2,1:T(8,128)(2,1)}), bf16[128,4,128]{0,2,1:T(8,128)(2,1)S(1)}, u32[]{:S(2)}, u32[]{:S(2)}) async-start(bf16[128,4,128]{0,2,1:T(8,128)(2,1)} %bitcast.11), calls=%async_computation.1 | async-start | bytes 262144 | tf_op jit(solution)/shard_map/all_to_all | solution.py:218
  173.2 8.8 all-to-all-start
  181.9 11.4 all-to-all-start.2
  186.0 11.1 copy-start.10
  186.2 11.0 copy-start.18
  197.2 8.5 copy-start.23
  202.1 35.0 %all-to-all-start.3 = ((bf16[4,128,512]{1,2,0:T(8,128)(2,1)}), bf16[4,128,512]{1,2,0:T(8,128)(2,1)S(1)}, u32[]{:S(2)}, u32[]{:S(2)}) async-start(bf16[4,128,512]{1,2,0:T(8,128)(2,1)} %copy.56), calls=%async_computation.3 | async-start | bytes 1048576 | tf_op jit(solution)/shard_map/all_to_all | solution.py:222
  205.6 1076.8 %reduce-scatter.11.cloned.1.call-start = ((), (), s32[]{:S(2)}) async-start(), calls=%async_computation.22 | async-start | bytes 2359296 | tf_op jit(solution)/shard_map/reduce_scatter | solution.py:295
  801.6 288.3 %copy-start.9 = (bf16[1,128,2048]{2,1,0:T(8,128)(2,1)S(1)}, bf16[1,128,2048]{2,1,0:T(8,128)(2,1)}, u32[]{:S(2)}) copy-start(bf16[1,128,2048]{2,1,0:T(8,128)(2,1)} %param.14) | copy-start | bytes 1572868
  1184.5 97.9 %reduce-scatter.9.cloned.1.call-start = ((), (), s32[]{:S(2)}) async-start(), calls=%async_computation.21 | async-start | bytes 2359296 | tf_op jit(solution)/shard_map/reduce_scatter | solution.py:292
  1210.4 135.4 %reduce-scatter.13.cloned.1.call-start = ((), (), s32[]{:S(2)}) async-start(), calls=%async_computation.23 | async-start | bytes 9437184 | tf_op jit(solution)/shard_map/reduce_scatter | solution.py:298
  1216.2 220.4 %reduce-scatter.7.cloned.1.call-start = ((), (), s32[]{:S(2)}) async-start(), calls=%async_computation.20 | async-start | bytes 9437184 | tf_op jit(solution)/shard_map/reduce_scatter | solution.py:289
  1238.4 524.4 %reduce-scatter.17.cloned.1.call-start = ((), (), s32[]{:S(2)}) async-start(), calls=%async_computation.25 | async-start | bytes 37748736 | tf_op jit(solution)/shard_map/reduce_scatter | solution.py:309
  1254.2 1149.5 %reduce-scatter.15.cloned.1.call-start = ((), (), s32[]{:S(2)}) async-start(), calls=%async_computation.24 | async-start | bytes 75497472 | tf_op jit(solution)/shard_map/reduce_scatter | solution.py:317
  1282.1 1121.7 %copy-start.24 = (u32[32]{0:T(128)S(1)}, u32[32]{0:T(128)}, u32[]{:S(2)}) copy-start(u32[32]{0:T(128)} %constant.105) | copy-start | bytes 388
  1282.1 1410.5 %all-reduce.7.cloned.1.call-start = ((), (), s32[]{:S(2)}) async-start(), calls=%async_computation.26 | async-start | bytes 30408704 | tf_op jit(solution)/shard_map/psum | solution.py:326
  2405.0 17.9 copy-start.14
  2405.0 17.9 copy-start.17
  2405.0 17.9 copy-start.7
  2422.9 7.6 copy-start.8
  2422.9 7.6 copy-start.12
  2692.6 12.0 copy-start.6
  2704.6 7.6 copy-start.20
  2704.6 8.4 copy-start.19
  (10 other events, 34.7 us)
Sparse Core Ops, SparseCore 0:
  9.6 31.8 all-gather.10
  43.1 28.5 all-gather.8
  73.3 81.5 all-gather.12
  156.4 80.6 all-gather.14
  239.1 562.4 all-gather.16
  803.1 286.8 all-gather.18
  1184.7 32.5 reduce-scatter.10
  1220.1 34.3 reduce-scatter.8
  1257.3 88.4 reduce-scatter.12
  1348.6 87.9 reduce-scatter.6
  1438.9 323.8 reduce-scatter.16
  1765.2 638.4 reduce-scatter.14
  2408.3 284.2 all-reduce.6
where the time goes:
time: 2730 us; the launch traced here: 2720 us
  waiting for transfers between devices  2320 us (85%)
  matrix products  209 us (8%)
  blocking collectives  85.1 us (3%)
  local copies, waits for them, and re-layouts  44.6 us (2%)
  other arithmetic  32.9 us (1%)
    reduce_scatter x1, waiting for transfers between devices, shards(): lax.psum_scatter(outer_rows(normed_two_low, grad_paired).astype(jnp.bfloa...  641 us
    all_gather x1, waiting for transfers between devices, shards(): lax.all_gather(paired_rows, 'fsdp', axis=0, tiled=True)  560 us
    reduce_scatter x1, waiting for transfers between devices, shards(): lax.psum_scatter(outer_rows(hidden, upstream_low).astype(jnp.bfloat16), '...  326 us
    all_gather x1, waiting for transfers between devices, shards(): full_down = lax.all_gather(w_down, 'fsdp', axis=0, tiled=True)  257 us
    psum x1, waiting for transfers between devices, shards(): lax.psum(shortened(attn_owned + (down_owned,) + pending), 'seq')  234 us
    reduce_scatter x1, waiting for transfers between devices, shards(): lax.psum_scatter(attn_terms[0].astype(jnp.bfloat16), 'fsdp', scatter_dime...  90.7 us
    all_gather x1, waiting for transfers between devices, shards(): lax.all_gather(w_query, 'fsdp', axis=0, tiled=True)  80.4 us
    dot_general x6, matrix products, product_back(): lax.dot_general(left_side, right_side, (((1,), (1,)), ((), ())), preferre...  65.5 us
  transfers between devices with their start and end apart: 17, of which 13 were waited for; matrix products, arithmetic and copies ran while one was open for 7% of the time, Pallas kernels for 0%

commit v1 on v0

v1 whole, which is shorter than its diff:
```python
import math

import jax
import jax.numpy as jnp
from jax import lax
from jax.sharding import Mesh
from jax.sharding import PartitionSpec as P

HD = 64
EPSILON = 1e-05
NEGATIVE = -1e30
SEQ = ("sa", "sb")
FS = ("p", "q", "c")
F32 = jnp.float32
BF16 = jnp.bfloat16


def frequencies():
    base_rate = 500000.0 ** (-jnp.arange(0, HD, 2, dtype=F32) / HD)
    wavelength = 2.0 * math.pi / base_rate
    smooth = (8192.0 / wavelength - 1.0) / 3.0
    middle_rate = (1.0 - smooth) * base_rate / 32.0 + smooth * base_rate
    return jnp.where(
        wavelength > 8192.0,
        base_rate / 32.0,
        jnp.where(wavelength < 2048.0, base_rate, middle_rate),
    )


def positions(doc_ids):
    index_all = jnp.arange(doc_ids.shape[0], dtype=jnp.int32)
    fresh = jnp.concatenate([jnp.ones((1,), dtype=bool), doc_ids[1:] != doc_ids[:-1]])
    first_index = lax.cummax(jnp.where(fresh, index_all, jnp.zeros_like(index_all)), axis=0)
    return index_all - first_index


def tables(pos_values):
    angles = pos_values.astype(F32)[:, None] * frequencies()[None, :]
    return (
        jnp.concatenate([jnp.cos(angles)] * 2, axis=1),
        jnp.concatenate([jnp.sin(angles)] * 2, axis=1),
    )


def rotation(values, cosine_table, sine_table):
    row_count = values.shape[0]
    shaped = values.reshape(row_count, -1, HD)
    half_size = HD // 2
    turned = jnp.concatenate([-shaped[..., half_size:], shaped[..., :half_size]], axis=-1)
    return (shaped * cosine_table[:, None, :] + turned * sine_table[:, None, :]).reshape(
        row_count, -1
    )


def product(left_side, right_side):
    return jnp.dot(left_side, right_side, preferred_element_type=F32)


def product_back(left_side, right_side):
    return lax.dot_general(
        left_side, right_side, (((1,), (1,)), ((), ())), preferred_element_type=F32
    )


def outer_rows(left_side, right_side):
    return lax.dot_general(
        left_side, right_side, (((0,), (0,)), ((), ())), preferred_element_type=F32
    )


def norm_factor(values):
    return lax.rsqrt(jnp.mean(values * values, axis=-1, keepdims=True) + EPSILON)


def norm_back(grad_normed, normed, factor):
    return factor * (grad_normed - normed * jnp.mean(grad_normed * normed, axis=-1, keepdims=True))


def swap(value, axes, size, distance):
    return lax.ppermute(value, axes, [(i, i ^ distance) for i in range(size)])


def low(value):
    return value.astype(BF16)


def layer_step(seq_size, fs_size):
    pairs = fs_size // 4

    def seq_swap(value, distance):
        return swap(value, SEQ, seq_size, distance)

    def gather_seq(block):
        if seq_size == 4:
            half = block.shape[0] // 2
            one, two = seq_swap(block, 1), seq_swap(block, 2)
            far = [seq_swap(two[:half], 1), seq_swap(one[half:], 2)]
            return [block, one, two, jnp.concatenate(far)]
        blocks, distance = [block], 1
        while distance < seq_size:
            got = seq_swap(jnp.stack(blocks), distance)
            blocks = blocks + [got[i] for i in range(distance)]
            distance *= 2
        return blocks

    def scatter_seq(blocks):
        if seq_size == 4:
            half = blocks[0].shape[0] // 2
            near, one, two, far = blocks
            far_low = low(far)
            to_two = seq_swap(far_low[:half], 1)
            to_one = seq_swap(far_low[half:], 2)
            one_top = seq_swap(low(one[:half]), 1)
            two_end = seq_swap(low(two[half:]), 2)
            one_end = seq_swap(low(one[half:].astype(F32) + to_one.astype(F32)), 1)
            two_top = seq_swap(low(two[:half].astype(F32) + to_two.astype(F32)), 2)
            return near.astype(F32) + jnp.concatenate(
                [
                    one_top.astype(F32) + two_top.astype(F32),
                    one_end.astype(F32) + two_end.astype(F32),
                ]
            )
        distance = seq_size // 2
        while distance:
            got = seq_swap(low(jnp.stack(blocks[distance:])), distance).astype(F32)
            blocks = [blocks[i].astype(F32) + got[i] for i in range(distance)]
            distance //= 2
        return blocks[0]

    def sum_all(value):
        for axes, size in ((FS, fs_size), (SEQ, seq_size)):
            distance = 1
            while distance < size:
                value = value + swap(value, axes, size, distance)
                distance *= 2
        return value

    def shards(
        tokens,
        documents,
        cotangent,
        w_query,
        w_key,
        w_value,
        w_output,
        w_gate,
        w_up,
        w_down,
        gain_attn,
        gain_mlp,
    ):
        rows, width = tokens.shape[1], tokens.shape[2]
        hidden_width = w_gate.shape[1]
        length = rows * seq_size
        own_seq = lax.axis_index(SEQ)
        own_fs = lax.axis_index(FS)

        def own_columns(weight):
            part = weight.shape[1] // seq_size
            return lax.dynamic_slice_in_dim(weight, own_seq * part, part, 1)

        def relative(blocks):
            return jnp.concatenate(
                [
                    lax.dynamic_index_in_dim(blocks, own_seq ^ k, 0, keepdims=True)
                    for k in range(seq_size)
                ]
            )

        tokens_own = tokens.reshape(rows, width)
        cot_own = cotangent.reshape(rows, width)
        doc_ids = documents.reshape(-1)
        token_blocks = gather_seq(tokens_own)
        attn_in = jnp.concatenate(
            [own_columns(w_query), own_columns(w_key), own_columns(w_value)], axis=1
        )
        full_qkv = lax.all_gather(attn_in, FS, axis=0, tiled=True)
        q_cols = w_query.shape[1] // seq_size
        k_cols = w_key.shape[1] // seq_size
        gains = jnp.stack([gain_attn, gain_mlp])
        gain_blocks, distance = gains[None], 1
        while distance < fs_size:
            gain_blocks = jnp.concatenate(
                [gain_blocks, swap(gain_blocks, FS, fs_size, distance)]
            )
            distance *= 2
        gain_full = jnp.concatenate(
            [
                lax.dynamic_index_in_dim(gain_blocks, own_fs ^ k, 0, keepdims=False)
                for k in range(fs_size)
            ],
            axis=1,
        ).astype(F32)
        full_gain_attn, full_gain_mlp = gain_full[0:1], gain_full[1:2]
        full_output = lax.all_gather(own_columns(w_output), FS, axis=0, tiled=True)
        out_cols = full_output.shape[1]
        output_rel = relative(full_output.reshape(seq_size, -1, out_cols))
        output_rel = output_rel.reshape(-1, out_cols)

        ff_rows = w_down.shape[0] // seq_size
        rows_in = w_gate.shape[0]

        def own_hidden(weight):
            shaped = weight.reshape(rows_in, fs_size, seq_size, ff_rows)
            part = lax.dynamic_index_in_dim(shaped, own_seq, 2, keepdims=False)
            return part.reshape(rows_in, pairs, 4, ff_rows)

        paired = jnp.stack([own_hidden(w_gate), own_hidden(w_up)], axis=1)
        paired = jnp.transpose(paired, (3, 0, 1, 2, 4))
        paired_send = jnp.stack(
            [
                jnp.stack([paired[:, :, :, k ^ p] for k in range(pairs)], axis=3)
                for p in range(pairs)
            ]
        ).reshape(fs_size, rows_in, -1)
        paired_full = lax.all_to_all(
            paired_send, FS, split_axis=0, concat_axis=0, tiled=True
        ).reshape(width, -1)
        down_own = lax.dynamic_slice_in_dim(w_down, own_seq * ff_rows, ff_rows, 0)
        down_full = jnp.concatenate(
            [down_own] + [swap(down_own, "p", pairs, k) for k in range(1, pairs)]
        )
        ff_own = ff_rows * pairs

        def gather_cube(block):
            beside = swap(block, "q", 2, 1)
            half = jnp.concatenate(gather_seq(block) + gather_seq(beside))
            return half, swap(half, "c", 2, 1)

        def scatter_cube(half, other):
            got = swap(low(other), "c", 2, 1)
            total = low(half + got.astype(F32)).reshape(2, seq_size, rows, width)
            across = scatter_seq([total[1, k] for k in range(seq_size)])
            back = swap(low(across), "q", 2, 1)
            return scatter_seq([total[0, k] for k in range(seq_size)]) + back.astype(F32)

        cot_halves = gather_cube(cot_own)

        sequence = jnp.concatenate(token_blocks).astype(F32)
        scale_one = norm_factor(sequence)
        normed_one = sequence * scale_one
        h_one = low(normed_one * full_gain_attn)
        order = relative(jnp.arange(length, dtype=jnp.int32).reshape(seq_size, rows)).reshape(-1)
        docs = relative(doc_ids.reshape(seq_size, rows)).reshape(-1)
        pos = relative(positions(doc_ids).reshape(seq_size, rows)).reshape(-1)
        cosine_table, sine_table = tables(pos)
        raw = product(h_one, full_qkv)
        group = q_cols // k_cols
        kv_heads = k_cols // HD
        queries = low(rotation(raw[:, :q_cols], cosine_table, sine_table))
        keys = low(rotation(raw[:, q_cols : q_cols + k_cols], cosine_table, sine_table))
        values = low(raw[:, q_cols + k_cols :])
        queries = queries.reshape(length, kv_heads, group, HD)
        keys = keys.reshape(length, kv_heads, HD)
        values = values.reshape(length, kv_heads, HD)
        visible = (order[None, :] <= order[:, None]) & (docs[None, :] == docs[:, None])
        factor = HD ** (-0.5)
        scores = jnp.einsum("qhgd,khd->hgqk", queries, keys, preferred_element_type=F32) * factor
        scores = jnp.where(visible[None, None], scores, NEGATIVE)
        largest = jnp.max(scores, axis=-1, keepdims=True)
        log_total = largest + jnp.log(jnp.sum(jnp.exp(scores - largest), axis=-1, keepdims=True))
        probs = jnp.exp(scores - log_total)
        probs_low = low(probs)
        mixed = low(
            jnp.einsum("hgqk,khd->qhgd", probs_low, values, preferred_element_type=F32)
        ).reshape(length, q_cols)
        def aligned(block, distance):
            parts = block.reshape(seq_size, rows, -1)
            return jnp.concatenate([parts[k ^ distance] for k in range(seq_size)])

        mixed_full = jnp.concatenate(
            [aligned(block, k) for k, block in enumerate(gather_seq(mixed))], axis=1
        )
        projected = product(mixed_full, output_rel).reshape(seq_size, rows, out_cols)

        def to_tokens(blocks):
            got = jnp.stack([blocks[0]] + [seq_swap(blocks[k], k) for k in range(1, seq_size)])
            return jnp.transpose(relative(got), (1, 0, 2)).reshape(rows, width)

        def to_columns(value):
            parts = [
                lax.dynamic_slice_in_dim(value, (own_seq ^ k) * out_cols, out_cols, 1)
                for k in range(seq_size)
            ]
            return jnp.concatenate(
                [parts[0]] + [seq_swap(parts[k], k) for k in range(1, seq_size)]
            )

        middle = tokens_own.astype(F32) + to_tokens(low(projected)).astype(F32)
        scale_two = norm_factor(middle)
        normed_two = middle * scale_two
        h_two = low(normed_two * full_gain_mlp)
        h_halves = gather_cube(h_two)

        outs, dhs, h_grads, down_grads = [], [], [], []
        for h_part, cot_part in zip(h_halves, cot_halves):
            both = product(h_part, paired_full)
            gate, upward = both[:, :ff_own], both[:, ff_own:]
            sigmoid_gate = jax.nn.sigmoid(gate)
            activated = gate * sigmoid_gate
            hidden = low(activated * upward)
            grad_hidden = product_back(cot_part, down_full)
            grad_up = low(grad_hidden * activated)
            grad_gate = low(
                grad_hidden * upward * sigmoid_gate * (1.0 + gate * (1.0 - sigmoid_gate))
            )
            grad_both = jnp.concatenate([grad_gate, grad_up], axis=1)
            dhs.append(product_back(grad_both, paired_full))
            outs.append(product(hidden, down_full))
            h_grads.append(outer_rows(h_part, grad_both))
            down_grads.append(outer_rows(hidden, cot_part))
        grad_normed_two = scatter_cube(*dhs)
        output = low(middle + scatter_cube(*outs))

        down_sum = (down_grads[0] + down_grads[1]).reshape(pairs, ff_rows, width)
        down_mine = down_sum[0]
        for k in range(1, pairs):
            down_mine = down_mine + swap(low(down_sum[k]), "p", pairs, k).astype(F32)
        down_out = lax.all_gather(low(down_mine), SEQ, axis=0, tiled=True).astype(F32)

        both_sum = low(h_grads[0] + h_grads[1]).reshape(fs_size, rows_in, -1)
        both_got = lax.all_to_all(both_sum, FS, split_axis=0, concat_axis=0, tiled=True)
        both_got = both_got.reshape(pairs, 4, rows_in, 2, pairs, ff_rows).astype(F32)
        both_mine = sum(
            jnp.stack([both_got[p, :, :, :, k ^ p] for k in range(pairs)]) for p in range(pairs)
        )
        both_mine = low(jnp.transpose(both_mine, (3, 2, 0, 1, 4)))
        both_out = lax.all_gather(both_mine, SEQ, axis=0)
        both_out = jnp.transpose(both_out, (1, 2, 3, 4, 0, 5)).reshape(2, rows_in, hidden_width)
        both_out = both_out.astype(F32)

        gain_two_grad = jnp.sum(grad_normed_two * normed_two, axis=0)
        grad_middle = cot_own.astype(F32) + norm_back(
            grad_normed_two * full_gain_mlp, normed_two, scale_two
        )
        middle_low = to_columns(low(grad_middle))
        grad_mixed = product_back(middle_low, output_rel).reshape(length, seq_size, q_cols)
        grad_heads = low(scatter_seq([aligned(grad_mixed[:, k], k) for k in range(seq_size)]))
        grad_heads = grad_heads.reshape(length, kv_heads, group, HD)
        grad_probs = jnp.einsum(
            "qhgd,khd->hgqk", grad_heads, values, preferred_element_type=F32
        )
        centre = jnp.sum(probs * grad_probs, axis=-1, keepdims=True)
        grad_scores = low(probs * (grad_probs - centre))
        query_grad = (
            jnp.einsum("hgqk,khd->qhgd", grad_scores, keys, preferred_element_type=F32) * factor
        )
        key_grad = (
            jnp.einsum("hgqk,qhgd->khd", grad_scores, queries, preferred_element_type=F32) * factor
        )
        value_grad = jnp.einsum(
            "hgqk,qhgd->khd", probs_low, grad_heads, preferred_element_type=F32
        )
        query_back = low(query_grad.reshape(length, -1)).astype(F32)
        key_back = low(key_grad.reshape(length, -1)).astype(F32)
        raw_grad = jnp.concatenate(
            [
                low(rotation(query_back, cosine_table, -sine_table)),
                low(rotation(key_back, cosine_table, -sine_table)),
                low(value_grad.reshape(length, -1)),
            ],
            axis=1,
        )
        grad_one_part = product_back(raw_grad, full_qkv)
        gain_one_grad = jnp.sum(grad_one_part * normed_one, axis=0)
        grad_normed_one = scatter_seq(
            [grad_one_part[k * rows : (k + 1) * rows] for k in range(seq_size)]
        )
        input_grad = grad_middle + norm_back(
            grad_normed_one * full_gain_attn, normed_one[:rows], scale_one[:rows]
        )
        output_grad = outer_rows(mixed_full, middle_low).reshape(seq_size, -1, out_cols)
        output_grad = relative(output_grad).reshape(width, out_cols)
        attn_grad = jnp.concatenate([outer_rows(h_one, raw_grad), output_grad], axis=1)
        attn_mine = lax.psum_scatter(low(attn_grad), FS, scatter_dimension=0, tiled=True)
        attn_out = lax.all_gather(attn_mine, SEQ, axis=0).astype(F32)

        def assembled(start, size):
            part = jnp.transpose(attn_out[:, :, start : start + size], (1, 0, 2))
            return part.reshape(rows_in, -1)

        gain_sums = sum_all(jnp.stack([gain_one_grad, gain_two_grad]))
        gain_mine = lax.dynamic_slice_in_dim(gain_sums, own_fs * rows_in, rows_in, 1)
        return (
            output.reshape(1, rows, width),
            low(input_grad).reshape(1, rows, width),
            assembled(0, q_cols),
            assembled(q_cols, k_cols),
            assembled(q_cols + k_cols, k_cols),
            assembled(q_cols + 2 * k_cols, out_cols),
            both_out[0],
            both_out[1],
            down_out,
            gain_mine[0],
            gain_mine[1],
        )

    return shards


def solution(mesh):
    seq_size, fs_size = mesh.shape["seq"], mesh.shape["fsdp"]
    fine = Mesh(
        mesh.devices.reshape(seq_size // 2, 2, fs_size // 4, 2, 2), SEQ + FS
    )
    token = P(FS, SEQ, None)
    weight = P(FS, None)
    gain = P(FS)
    return jax.shard_map(
        layer_step(seq_size, fs_size),
        mesh=fine,
        in_specs=(token, weight, token) + (weight,) * 7 + (gain, gain),
        out_specs=(token, token) + (weight,) * 7 + (gain, gain),
        check_vma=False,
    )
```

time: 2730 us -> 1000 us (0.37)
  waiting for transfers between devices: 2320 us -> 476 us
  local copies, waits for them, and re-layouts: 44.6 us -> 215 us
  matrix products: 209 us -> 106 us
  blocking collectives: 85.1 us -> 0 us
  starting transfers between devices: 15.3 us -> 97.9 us
  other arithmetic: 32.9 us -> 86.1 us
    reduce_scatter x6 -> x1, waiting for transfers between devices: 1120 us -> 0.02 us  [shards(): lax.psum_scatter(low(attn_grad), FS, scatter_dimension=0, tiled=True)]
    all_gather x6 -> x5, waiting for transfers between devices: 948 us -> 25.5 us  [the longest x1 25.5 us: shards(): both_out = lax.all_gather(both_mine, SEQ, axis=0)]
    ppermute x0 -> x84, waiting for transfers between devices: none -> 451 us  [swap(): return lax.ppermute(value, axes, [(i, i ^ distance) for i in range(size)])]
    psum x1 -> x0, waiting for transfers between devices: 234 us -> none  [shards(): lax.psum(shortened(attn_owned + (down_owned,) + pending), 'seq')]
    ppermute x0 -> x84, starting transfers between devices: none -> 86.7 us  [swap(): return lax.ppermute(value, axes, [(i, i ^ distance) for i in range(size)])]
    unnamed x55 -> x157, local copies, waits for them, and re-layouts: 5.77 us -> 77.6 us
    dot_general x12, matrix products: 84.2 us -> 43 us  [the longest x6 30.2 us: product(): return jnp.dot(left_side, right_side, preferred_element_type=F32)]
    slice x2 -> x37, local copies, waits for them, and re-layouts: 12 us -> 49.3 us  [the longest x2 21.2 us: shards(): both_out[1]]
  transfers between devices with their start and end apart: 17 -> 92, of which waited for: 13 -> 47; matrix products, arithmetic and copies ran while one was open for 7% -> 33% of each run, Pallas kernels for 0% -> 0%
where the time goes in v1:
time: 1000 us; the launch traced here: 997 us
  waiting for transfers between devices  476 us (48%)
  local copies, waits for them, and re-layouts  215 us (22%)
  matrix products  106 us (11%)
  starting transfers between devices  97.9 us (10%)
  other arithmetic  86.1 us (9%)
  between operations  16.1 us (2%)
    ppermute x84, waiting for transfers between devices, swap(): return lax.ppermute(value, axes, [(i, i ^ distance) for i in range(size)])  451 us
    ppermute x84, starting transfers between devices, swap(): return lax.ppermute(value, axes, [(i, i ^ distance) for i in range(size)])  86.7 us
    unnamed x157, local copies, waits for them, and re-layouts  77.6 us
    dot_general x6, matrix products, product_back(): lax.dot_general(left_side, right_side, (((1,), (1,)), ((), ())), preferre...  33.4 us
    dot_general x6, matrix products, product(): return jnp.dot(left_side, right_side, preferred_element_type=F32)  30.2 us
    dot_general x6, matrix products, outer_rows(): lax.dot_general(left_side, right_side, (((0,), (0,)), ((), ())), preferre...  29.8 us
    all_gather x1, waiting for transfers between devices, shards(): both_out = lax.all_gather(both_mine, SEQ, axis=0)  25.5 us
    slice x2, local copies, waits for them, and re-layouts, shards(): both_out[1]  21.2 us
  transfers between devices with their start and end apart: 92, of which 47 were waited for; matrix products, arithmetic and copies ran while one was open for 33% of the time, Pallas kernels for 0%

profile of v1, /device:TPU:0, one launch (start us, length us, event | category | flops | bytes accessed | tf_op | source)
XLA Modules:
  0.0 997.4 jit_solution(5480307867645544098)
XLA Ops:
  16.6 6.5 copy.97
  35.3 7.3 copy.99
  54.8 78.8 %collective-permute-done.5 = bf16[2,2,256]{2,1,0:T(2,128)(2,1)S(1)} collective-permute-done((bf16[2,2,256]{2,1,0:T(2,128)(2,1)S(1)}, bf16[2,2,256]{2,1,0:T(2,128)(2,1)S(1)}, u32[]{:S(2)}, u32[]{:S(2)}) %collective-permute-start.5) | collective-permute-done | bytes 2080 | tf_op jit(solution)/shard_map/ppermute | solution.py:80
  140.4 18.8 %collective-permute-done.6 = bf16[4,2,256]{2,1,0:T(2,128)(2,1)} collective-permute-done((bf16[4,2,256]{2,1,0:T(2,128)(2,1)S(1)}, bf16[4,2,256]{2,1,0:T(2,128)(2,1)}, u32[]{:S(2)}, u32[]{:S(2)}) %collective-permute-start.6) | collective-permute-done | bytes 4128 | tf_op jit(solution)/shard_map/ppermute | solution.py:80
  224.3 9.1 collective-permute-done.7
  240.0 11.2 %maximum_maximum_fusion = bf16[512,2048]{0,1:T(8,128)(2,1)} fusion(bf16[128,512]{0,1:T(8,128)(2,1)S(1)} %get-tuple-element.139, bf16[128,512]{0,1:T(8,128)(2,1)S(1)} %get-tuple-element.138, bf16[128,512]{0,1:T(8,128)(2,1)S(1)} %get-tuple-element.137, bf16[128,512]{0,1:T(8,128)(2,1)S(1)} %get-tuple-element.136, bf16[256,512]{0,1:T(8,128)(2,1)S(1)} %get-tuple-element.133, ...), kind=kLoop, calls=%fused_computation.36 | loop fusion | flops 29360128 | bytes 4194304 | tf_op jit(solution)/shard_map/concatenate | solution.py:271
  293.7 8.9 collective-permute-done.16
  306.5 8.1 collective-permute-done.20
  346.3 7.8 fusion.93
  354.2 32.8 %collective-permute-done.23 = bf16[256,2048]{1,0:T(8,128)(2,1)} collective-permute-done((bf16[256,2048]{1,0:T(8,128)(2,1)}, bf16[256,2048]{1,0:T(8,128)(2,1)}, u32[]{:S(2)}, u32[]{:S(2)}) %collective-permute-start.23) | collective-permute-done | bytes 1048608 | tf_op jit(solution)/shard_map/ppermute | solution.py:80
  387.0 6.8 multiply_convert_fusion.2
  398.8 6.4 fusion.92
  405.2 6.9 multiply_convert_fusion.4
  506.4 6.7 pad_maximum_fusion.7
  532.1 7.3 fusion.11
  539.5 9.6 add_convert_fusion
  549.1 6.4 copy.112
  572.7 151.8 %collective-permute-done.78 = bf16[256,2048]{1,0:T(8,128)(2,1)S(1)} collective-permute-done((bf16[256,2048]{1,0:T(8,128)(2,1)S(1)}, bf16[256,2048]{1,0:T(8,128)(2,1)S(1)}, u32[]{:S(2)}, u32[]{:S(2)}) %collective-permute-start.78) | collective-permute-done | bytes 1048608 | tf_op jit(solution)/shard_map/ppermute | solution.py:80
  737.2 7.1 collective-permute-done.25
  754.8 7.8 collective-permute-done.27
  765.5 7.5 collective-permute-done.33
  805.0 8.4 multiply_reduce_fusion
  817.0 12.4 %collective-permute-done.80 = f32[2,2048]{1,0:T(2,128)S(1)} collective-permute-done((f32[2,2048]{1,0:T(2,128)S(1)}, f32[2,2048]{1,0:T(2,128)S(1)}, u32[]{:S(2)}, u32[]{:S(2)}) %collective-permute-start.80) | collective-permute-done | bytes 16416 | tf_op jit(solution)/shard_map/ppermute | solution.py:80
  849.3 14.8 %collective-permute-done.76 = bf16[64,2048]{1,0:T(8,128)(2,1)S(1)} collective-permute-done((bf16[64,2048]{1,0:T(8,128)(2,1)S(1)}, bf16[64,2048]{1,0:T(8,128)(2,1)S(1)}, u32[]{:S(2)}, u32[]{:S(2)}) %collective-permute-start.76) | collective-permute-done | bytes 262176 | tf_op jit(solution)/shard_map/ppermute | solution.py:80
  869.1 6.7 convert_element_type.569
  875.7 25.5 %all-gather.16.cloned.1.call-done = bf16[8,256,2,4,256]{1,4,0,3,2:T(8,128)(2,1)} async-done(((bf16[2,256,2,4,256]{1,4,0,3,2:T(8,128)(2,1)}), bf16[8,256,2,4,256]{1,4,0,3,2:T(8,128)(2,1)}) %all-gather.16.cloned.1.call-update) | async-done | bytes 8388624 | tf_op jit(solution)/shard_map/all_gather | solution.py:328
  901.2 13.3 %copy.116 = f32[8,256,2,4,256]{4,1,3,2,0:T(8,128)} copy(bf16[8,256,2,4,256]{1,4,0,3,2:T(8,128)(2,1)} %all-gather.16.cloned.1.call-done) | data formatting | bytes 25165824 | tf_op jit(solution)/shard_map/convert_element_type | solution.py:330
  914.6 11.3 %fusion.80 = (f32[1,256,2,4,4,256]{5,1,3,2,0,4:T(8,128)}, f32[1,256,2,4,4,256]{5,1,3,2,0,4:T(8,128)}) fusion(f32[2,256,2,4,4,256]{5,1,3,2,0,4:T(8,128)} %bitcast.395), kind=kLoop, calls=%fused_computation.334 | loop fusion | bytes 33554432 | tf_op jit(solution)/shard_map/slice | solution.py:392
  925.9 10.0 copy.117
  935.9 8.9 copy.119
  944.8 9.9 copy.118
  954.6 8.9 copy.120
  (509 shorter events, 437.5 us)
Async XLA Ops:
  7.2 164.5 %all-gather.8.cloned.1.call-start = ((), (), s32[]{:S(2)}) async-start(), calls=%async_computation.3 | async-start | bytes 3538944 | tf_op jit(solution)/shard_map/all_gather | solution.py:177
  10.1 152.5 %collective-permute-start = (bf16[128,2048]{1,0:T(8,128)(2,1)}, bf16[128,2048]{1,0:T(8,128)(2,1)}, u32[]{:S(2)}, u32[]{:S(2)}) collective-permute-start(bf16[128,2048]{1,0:T(8,128)(2,1)} %bitcast.437), channel_id=1, source_target_pairs={{0,8},{8,0},{16,24},{24,16},{1,9},{9,1},{17,25},{25,17},{2,10},{10... | collective-permute-start | bytes 1572872 | tf_op jit(solution)/shard_map/ppermute | solution.py:80
  13.1 147.0 %collective-permute-start.1 = (bf16[128,2048]{1,0:T(8,128)(2,1)}, bf16[128,2048]{1,0:T(8,128)(2,1)}, u32[]{:S(2)}, u32[]{:S(2)}) collective-permute-start(bf16[128,2048]{1,0:T(8,128)(2,1)} %bitcast.438), channel_id=1, source_target_pairs={{0,16},{8,24},{16,0},{24,8},{1,17},{9,25},{17,1},{25,9},{2,18},{10... | collective-permute-start | bytes 1572872 | tf_op jit(solution)/shard_map/ppermute | solution.py:80
  14.7 199.6 %collective-permute-start.39 = (bf16[128,2048]{1,0:T(8,128)(2,1)}, bf16[128,2048]{1,0:T(8,128)(2,1)}, u32[]{:S(2)}, u32[]{:S(2)}) collective-permute-start(bf16[128,2048]{1,0:T(8,128)(2,1)} %bitcast.75), channel_id=1, source_target_pairs={{0,8},{8,0},{16,24},{24,16},{1,9},{9,1},{17,25},{25,17},{2,10},{10... | collective-permute-start | bytes 1572872 | tf_op jit(solution)/shard_map/ppermute | solution.py:80
  15.2 196.9 %collective-permute-start.40 = (bf16[128,2048]{1,0:T(8,128)(2,1)}, bf16[128,2048]{1,0:T(8,128)(2,1)}, u32[]{:S(2)}, u32[]{:S(2)}) collective-permute-start(bf16[128,2048]{1,0:T(8,128)(2,1)} %bitcast.75), channel_id=1, source_target_pairs={{0,16},{8,24},{16,0},{24,8},{1,17},{9,25},{17,1},{25,9},{2,18},{10... | collective-permute-start | bytes 1572872 | tf_op jit(solution)/shard_map/ppermute | solution.py:80
  16.6 35.4 %collective-permute-start.4 = (bf16[1,2,256]{2,1,0:T(2,128)(2,1)S(1)}, bf16[1,2,256]{2,1,0:T(2,128)(2,1)S(1)}, u32[]{:S(2)}, u32[]{:S(2)}) collective-permute-start(bf16[1,2,256]{2,1,0:T(2,128)(2,1)S(1)} %maximum_bitcast_fusion.1), channel_id=1, source_target_pairs={{0,1},{1,0},{2,3},{3,2},{4,5},{5,4},{6,7},{7,6},{8,9},{9,8},{10,11... | collective-permute-start | bytes 3080 | tf_op jit(solution)/shard_map/ppermute | solution.py:80
  42.6 297.3 %all-to-all-start = ((bf16[8,256,1024]{1,2,0:T(8,128)(2,1)}), bf16[8,256,1024]{1,2,0:T(8,128)(2,1)}, u32[]{:S(2)}, u32[]{:S(2)}) async-start(bf16[8,256,1024]{1,2,0:T(8,128)(2,1)} %bitcast.398), calls=%async_computation | async-start | bytes 8388608 | tf_op jit(solution)/shard_map/all_to_all | solution.py:216
  48.1 167.9 %all-gather.10.cloned.1.call-start = ((), (), s32[]{:S(2)}) async-start(), calls=%async_computation.4 | async-start | bytes 2359296 | tf_op jit(solution)/shard_map/all_gather | solution.py:195
  49.8 785.1 %reduce-scatter.2.cloned.1.call-start = ((), (), s32[]{:S(2)}) async-start(), calls=%async_computation.5 | async-start | bytes 5898240 | tf_op jit(solution)/shard_map/reduce_scatter | solution.py:375
  52.0 81.6 %collective-permute-start.5 = (bf16[2,2,256]{2,1,0:T(2,128)(2,1)S(1)}, bf16[2,2,256]{2,1,0:T(2,128)(2,1)S(1)}, u32[]{:S(2)}, u32[]{:S(2)}) collective-permute-start(bf16[2,2,256]{2,1,0:T(2,128)(2,1)S(1)} %pad_maximum_fusion.31), channel_id=1, source_target_pairs={{0,2},{1,3},{2,0},{3,1},{4,6},{5,7},{6,4},{7,5},{8,10},{9,11},{10,... | collective-permute-start | bytes 6152 | tf_op jit(solution)/shard_map/ppermute | solution.py:80
  133.6 25.6 %collective-permute-start.6 = (bf16[4,2,256]{2,1,0:T(2,128)(2,1)S(1)}, bf16[4,2,256]{2,1,0:T(2,128)(2,1)}, u32[]{:S(2)}, u32[]{:S(2)}) collective-permute-start(bf16[4,2,256]{2,1,0:T(2,128)(2,1)S(1)} %pad_maximum_fusion.30), channel_id=1, source_target_pairs={{0,4},{1,5},{2,6},{3,7},{4,0},{5,1},{6,2},{7,3},{8,12},{9,13},{10,... | collective-permute-start | bytes 12296 | tf_op jit(solution)/shard_map/ppermute | solution.py:80
  159.2 117.7 %collective-permute-start.43 = (bf16[128,2048]{1,0:T(8,128)(2,1)}, bf16[128,2048]{1,0:T(8,128)(2,1)}, u32[]{:S(2)}, u32[]{:S(2)}) collective-permute-start(bf16[128,2048]{1,0:T(8,128)(2,1)} %bitcast.75), channel_id=1, source_target_pairs={{0,2},{2,0},{1,3},{3,1},{4,6},{6,4},{5,7},{7,5},{8,10},{10,8},{9,1... | collective-permute-start | bytes 1572872 | tf_op jit(solution)/shard_map/ppermute | solution.py:80
  213.7 64.8 %collective-permute-start.41 = (bf16[64,2048]{1,0:T(8,128)(2,1)}, bf16[64,2048]{1,0:T(8,128)(2,1)}, u32[]{:S(2)}, u32[]{:S(2)}) collective-permute-start(bf16[64,2048]{1,0:T(8,128)(2,1)} %slice.744), channel_id=1, source_target_pairs={{0,8},{8,0},{16,24},{24,16},{1,9},{9,1},{17,25},{25,17},{2,10},{10... | collective-permute-start | bytes 786440 | tf_op jit(solution)/shard_map/ppermute | solution.py:80
  276.9 49.0 %collective-permute-start.44 = (bf16[128,2048]{1,0:T(8,128)(2,1)}, bf16[128,2048]{1,0:T(8,128)(2,1)S(1)}, u32[]{:S(2)}, u32[]{:S(2)}) collective-permute-start(bf16[128,2048]{1,0:T(8,128)(2,1)} %collective-permute-done.43), channel_id=1, source_target_pairs={{0,8},{8,0},{16,24},{24,16},{1,9},{9,1},{17,25},{25,17},{2,10},{10... | collective-permute-start | bytes 1572872 | tf_op jit(solution)/shard_map/ppermute | solution.py:80
  278.5 46.6 %collective-permute-start.45 = (bf16[128,2048]{1,0:T(8,128)(2,1)}, bf16[128,2048]{1,0:T(8,128)(2,1)S(1)}, u32[]{:S(2)}, u32[]{:S(2)}) collective-permute-start(bf16[128,2048]{1,0:T(8,128)(2,1)} %collective-permute-done.43), channel_id=1, source_target_pairs={{0,16},{8,24},{16,0},{24,8},{1,17},{9,25},{17,1},{25,9},{2,18},{10... | collective-permute-start | bytes 1572872 | tf_op jit(solution)/shard_map/ppermute | solution.py:80
  323.3 23.1 %collective-permute-start.24 = (bf16[1024,2048]{1,0:T(8,128)(2,1)}, bf16[1024,2048]{1,0:T(8,128)(2,1)}, u32[]{:S(2)}, u32[]{:S(2)}) collective-permute-start(bf16[1024,2048]{1,0:T(8,128)(2,1)} %constant_dynamic-update-slice_fusion.13), channel_id=1, source_target_pairs={{0,1},{1,0},{2,3},{3,2},{4,5},{5,4},{6,7},{7,6},{8,9},{9,8},{10,11... | collective-permute-start | bytes 12582920 | tf_op jit(solution)/shard_map/ppermute | solution.py:80
  335.4 51.6 %collective-permute-start.48 = (bf16[1024,2048]{1,0:T(8,128)(2,1)}, bf16[1024,2048]{1,0:T(8,128)(2,1)}, u32[]{:S(2)}, u32[]{:S(2)}) collective-permute-start(bf16[1024,2048]{1,0:T(8,128)(2,1)} %constant_dynamic-update-slice_fusion.23), channel_id=1, source_target_pairs={{0,1},{1,0},{2,3},{3,2},{4,5},{5,4},{6,7},{7,6},{8,9},{9,8},{10,11... | collective-permute-start | bytes 12582920 | tf_op jit(solution)/shard_map/ppermute | solution.py:80
  337.8 49.3 %collective-permute-start.23 = (bf16[256,2048]{1,0:T(8,128)(2,1)}, bf16[256,2048]{1,0:T(8,128)(2,1)}, u32[]{:S(2)}, u32[]{:S(2)}) collective-permute-start(bf16[256,2048]{1,0:T(8,128)(2,1)} %constant_dynamic-slice_fusion.10), channel_id=1, source_target_pairs={{0,4},{4,0},{1,5},{5,1},{2,6},{6,2},{3,7},{7,3},{8,12},{12,8},{9,1... | collective-permute-start | bytes 3145736 | tf_op jit(solution)/shard_map/ppermute | solution.py:80
  478.7 35.1 %collective-permute-start.71 = (bf16[256,512]{0,1:T(8,128)(2,1)}, bf16[256,512]{0,1:T(8,128)(2,1)}, u32[]{:S(2)}, u32[]{:S(2)}) collective-permute-start(bf16[256,512]{0,1:T(8,128)(2,1)} %pad_maximum_fusion.23), channel_id=1, source_target_pairs={{0,16},{8,24},{16,0},{24,8},{1,17},{9,25},{17,1},{25,9},{2,18},{10... | collective-permute-start | bytes 786440 | tf_op jit(solution)/shard_map/ppermute | solution.py:80
  484.1 31.1 %collective-permute-start.66 = (bf16[256,512]{0,1:T(8,128)(2,1)}, bf16[256,512]{0,1:T(8,128)(2,1)}, u32[]{:S(2)}, u32[]{:S(2)}) collective-permute-start(bf16[256,512]{0,1:T(8,128)(2,1)} %pad_maximum_fusion.20), channel_id=1, source_target_pairs={{0,8},{8,0},{16,24},{24,16},{1,9},{9,1},{17,25},{25,17},{2,10},{10... | collective-permute-start | bytes 786440 | tf_op jit(solution)/shard_map/ppermute | solution.py:80
  555.5 170.3 %all-to-all-start.1 = ((bf16[8,256,1024]{1,2,0:T(8,128)(2,1)}), bf16[8,256,1024]{1,2,0:T(8,128)(2,1)}, u32[]{:S(2)}, u32[]{:S(2)}) async-start(bf16[8,256,1024]{1,2,0:T(8,128)(2,1)} %copy.112), calls=%async_computation.2 | async-start | bytes 8388608 | tf_op jit(solution)/shard_map/all_to_all | solution.py:322
  560.1 309.0 %all-gather.12.cloned.1.call-start = ((), (), s32[]{:S(2)}) async-start(), calls=%async_computation.6 | async-start | bytes 5242880 | tf_op jit(solution)/shard_map/all_gather | solution.py:319
  569.9 154.5 %collective-permute-start.78 = (bf16[256,2048]{1,0:T(8,128)(2,1)S(1)}, bf16[256,2048]{1,0:T(8,128)(2,1)S(1)}, u32[]{:S(2)}, u32[]{:S(2)}) collective-permute-start(bf16[256,2048]{1,0:T(8,128)(2,1)S(1)} %slice.926), channel_id=1, source_target_pairs={{0,4},{4,0},{1,5},{5,1},{2,6},{6,2},{3,7},{7,3},{8,12},{12,8},{9,1... | collective-permute-start | bytes 3145736 | tf_op jit(solution)/shard_map/ppermute | solution.py:80
  725.8 175.4 %all-gather.16.cloned.1.call-start = ((), (), s32[]{:S(2)}) async-start(), calls=%async_computation.8 | async-start | bytes 10485760 | tf_op jit(solution)/shard_map/all_gather | solution.py:328
  731.9 231.6 %all-gather.14.cloned.1.call-start = ((), (), s32[]{:S(2)}) async-start(), calls=%async_computation.7 | async-start | bytes 3276800 | tf_op jit(solution)/shard_map/all_gather | solution.py:376
  752.8 23.9 %collective-permute-start.29 = (bf16[64,2048]{1,0:T(8,128)(2,1)S(1)}, bf16[64,2048]{1,0:T(8,128)(2,1)S(1)}, u32[]{:S(2)}, u32[]{:S(2)}) collective-permute-start(bf16[64,2048]{1,0:T(8,128)(2,1)S(1)} %get-tuple-element.75), channel_id=1, source_target_pairs={{0,16},{8,24},{16,0},{24,8},{1,17},{9,25},{17,1},{25,9},{2,18},{10... | collective-permute-start | bytes 786440 | tf_op jit(solution)/shard_map/ppermute | solution.py:80
  753.5 34.6 %collective-permute-start.37 = (bf16[64,2048]{1,0:T(8,128)(2,1)}, bf16[64,2048]{1,0:T(8,128)(2,1)}, u32[]{:S(2)}, u32[]{:S(2)}) collective-permute-start(bf16[64,2048]{1,0:T(8,128)(2,1)} %get-tuple-element.70), channel_id=1, source_target_pairs={{0,16},{8,24},{16,0},{24,8},{1,17},{9,25},{17,1},{25,9},{2,18},{10... | collective-permute-start | bytes 786440 | tf_op jit(solution)/shard_map/ppermute | solution.py:80
  780.0 34.9 %collective-permute-start.31 = (bf16[64,2048]{1,0:T(8,128)(2,1)}, bf16[64,2048]{1,0:T(8,128)(2,1)S(1)}, u32[]{:S(2)}, u32[]{:S(2)}) collective-permute-start(bf16[64,2048]{1,0:T(8,128)(2,1)} %get-tuple-element.74), channel_id=1, source_target_pairs={{0,16},{8,24},{16,0},{24,8},{1,17},{9,25},{17,1},{25,9},{2,18},{10... | collective-permute-start | bytes 786440 | tf_op jit(solution)/shard_map/ppermute | solution.py:80
  781.1 53.9 %collective-permute-start.26 = (bf16[64,2048]{1,0:T(8,128)(2,1)}, bf16[64,2048]{1,0:T(8,128)(2,1)}, u32[]{:S(2)}, u32[]{:S(2)}) collective-permute-start(bf16[64,2048]{1,0:T(8,128)(2,1)} %get-tuple-element.69), channel_id=1, source_target_pairs={{0,8},{8,0},{16,24},{24,16},{1,9},{9,1},{17,25},{25,17},{2,10},{10... | collective-permute-start | bytes 786440 | tf_op jit(solution)/shard_map/ppermute | solution.py:80
  792.7 24.3 %collective-permute-start.30 = (bf16[64,2048]{1,0:T(8,128)(2,1)}, bf16[64,2048]{1,0:T(8,128)(2,1)S(1)}, u32[]{:S(2)}, u32[]{:S(2)}) collective-permute-start(bf16[64,2048]{1,0:T(8,128)(2,1)} %get-tuple-element.80), channel_id=1, source_target_pairs={{0,8},{8,0},{16,24},{24,16},{1,9},{9,1},{17,25},{25,17},{2,10},{10... | collective-permute-start | bytes 786440 | tf_op jit(solution)/shard_map/ppermute | solution.py:80
  798.2 38.3 %collective-permute-start.28 = (bf16[64,2048]{1,0:T(8,128)(2,1)}, bf16[64,2048]{1,0:T(8,128)(2,1)}, u32[]{:S(2)}, u32[]{:S(2)}) collective-permute-start(bf16[64,2048]{1,0:T(8,128)(2,1)} %get-tuple-element.77), channel_id=1, source_target_pairs={{0,16},{8,24},{16,0},{24,8},{1,17},{9,25},{17,1},{25,9},{2,18},{10... | collective-permute-start | bytes 786440 | tf_op jit(solution)/shard_map/ppermute | solution.py:80
  814.8 51.1 %collective-permute-start.38 = (bf16[128,2048]{1,0:T(8,128)(2,1)S(1)}, bf16[128,2048]{1,0:T(8,128)(2,1)S(1)}, u32[]{:S(2)}, u32[]{:S(2)}) collective-permute-start(bf16[128,2048]{1,0:T(8,128)(2,1)S(1)} %fusion.26), channel_id=1, source_target_pairs={{0,2},{2,0},{1,3},{3,1},{4,6},{6,4},{5,7},{7,5},{8,10},{10,8},{9,1... | collective-permute-start | bytes 1572872 | tf_op jit(solution)/shard_map/ppermute | solution.py:80
  (120 other events, 1494.5 us)
Sparse Core Ops, SparseCore 0:
  10.3 40.9 all-gather.7
  53.4 49.1 all-gather.9
  532.2 87.7 reduce-scatter.1
  725.9 73.7 all-gather.11
  802.0 99.1 all-gather.15
  902.9 39.4 all-gather.13
